TPU v7x, 512 devices: a whole 4x8x8 slice. The times are simulated.
512 devices in a mesh: va: 32 (over x_lo, y, core), vb: 16 (over x_hi, z).
Axes of the slice: x: 4 (x_hi: 2, x_lo: 2; x = x_hi * 2 + x_lo), y: 8, z: 8, core: 2. Of those that a mesh axis runs over, the one named last changes fastest.
Arguments:
- amplitudes: bfloat16 [1024, 8, 65536], P('va', None, 'vb'), may hold values from -6 to 6
- integrals: bfloat16 [1024, 65536], P('va', 'vb'), may hold values from -0.125 to 0.125
- irrep_virt: int32 [1024], replicated, may hold values from 0 to 7
- irrep_occ: int32 [64], replicated, may hold values from 0 to 7, as said below
- irrep_slab: int32 [8], replicated, may hold values from 0 to 7
Outputs:
- cycle_term: bfloat16 [1024, 8192], P('vb', 'va')
Inputs may be any that keep to these rules, and one draw needn't show every extreme that they name: `irrep_virt`: D2h irrep labels. `irrep_occ`: D2h irrep labels; each aligned group of 8 consecutive orbitals k holds every label exactly once. `irrep_slab`: D2h irrep labels.
All inputs are finite; a program needn't handle non-finite values.
Results may differ from a plain program's by a relative error of at most 0.0015.
Values may be sent and summed in bfloat16 or wider, within the bound.
No kernel may reach another device: no remote copies, remote signals or barrier semaphores. Data moves between devices by JAX's collectives and lax.ppermute only.
A program may use at most 64 MiB of HBM per device.

v0:
```python
import jax
import jax.numpy as jnp
from jax import lax
from jax.sharding import PartitionSpec as P


def per_device(amplitudes, integrals, irrep_virt, irrep_occ, irrep_slab):
    a_rows, slab_count, pair_local = amplitudes.shape
    occ_count = irrep_occ.shape[0]
    c_local = pair_local // occ_count
    irr_first = lax.dynamic_slice_in_dim(irrep_virt, lax.axis_index("va") * a_rows, a_rows, 0)
    irr_second = lax.dynamic_slice_in_dim(irrep_virt, lax.axis_index("vb") * c_local, c_local, 0)
    pair_tag = jnp.bitwise_xor(irr_second[:, None], irrep_occ[None, :]).reshape(pair_local)
    left_tag = jnp.bitwise_xor(irr_first[:, None], irrep_slab[None, :])
    amp_sym = jnp.where(
        left_tag[:, :, None] == pair_tag[None, None, :], amplitudes, jnp.zeros_like(amplitudes)
    )
    flat_amp = amp_sym.reshape(a_rows * slab_count, pair_local)
    row_tag = jnp.bitwise_xor(irrep_virt, irrep_occ[0])
    gathered = lax.all_gather(integrals, "va", axis=0, tiled=True)
    int_sym = jnp.where(row_tag[:, None] == pair_tag[None, :], gathered, jnp.zeros_like(gathered))
    summed = lax.psum_scatter(
        lax.dot_general(
            int_sym, flat_amp, (((1,), (1,)), ((), ())), preferred_element_type=jnp.float32
        ),
        "vb",
        scatter_dimension=0,
        tiled=True,
    )
    return summed.astype(jnp.bfloat16)


def solution(mesh):
    placed = (P("va", None, "vb"), P("va", "vb"), P(), P(), P())
    return jax.shard_map(
        per_device, mesh=mesh, in_specs=placed, out_specs=P("vb", "va"), check_vma=False
    )
```

profile of v0, /device:TPU:8, one launch (start us, length us, event | category | flops | bytes accessed | tf_op | source)
XLA Modules:
  0.0 310.7 jit_solution(5064224351063463156)
XLA Ops:
  6.5 0.0 all-gather.2.cloned.1.call-start
  6.5 0.7 all-gather.2.cloned.1.call-update
  7.3 0.0 reduce-scatter.2.cloned.1.call-start
  7.3 0.8 dynamic_slice.7
  8.1 0.8 dynamic_slice.6
  8.8 0.7 broadcast_xor_fusion
  9.6 0.1 xor.52
  9.6 1.3 broadcast_xor_fusion.2
  11.0 0.7 broadcast_xor_fusion.1
  11.7 76.8 %all-gather.2.cloned.1.call-done = bf16[1024,4096]{1,0:T(8,128)(2,1)} async-done(((bf16[32,4096]{1,0:T(8,128)(2,1)}), bf16[1024,4096]{1,0:T(8,128)(2,1)}) %all-gather.2.cloned.1.call-update) | async-done | bytes 8388624 | tf_op jit(solution)/shard_map/all_gather | solution.py:20
  88.5 8.0 %fusion = f32[1024,256]{1,0:T(8,128)} fusion(bf16[1024,4096]{1,0:T(8,128)(2,1)} %all-gather.2.cloned.1.call-done, s32[4096]{0:T(1024)S(1)} %xor.52, s32[1024]{0:T(1024)S(1)} %broadcast_xor_fusion.2, bf16[32,8,4096]{2,1,0:T(8,128)(2,1)} %param.5, s32[32,8]{1,0:T(8,128)S(1)} %broadcast_xor_fusion.1), kind=kOutput, calls=%fused_computation.1 | convolution fusion | flops 2157969408 | bytes 11555840 | tf_op jit(solution)/shard_map/dot_general | solution.py:23
  96.5 0.0 reduce-scatter.2.cloned.1.call-update
  96.6 205.8 %reduce-scatter.2.cloned.1.call-done = f32[64,256]{1,0:T(8,128)} async-done(((f32[1024,256]{1,0:T(8,128)}), f32[64,256]{1,0:T(8,128)}) %reduce-scatter.2.cloned.1.call-update) | async-done | bytes 65552 | tf_op jit(solution)/shard_map/reduce_scatter | solution.py:22
  302.4 1.5 convert_element_type.3
Async XLA Ops:
  6.5 82.0 %all-gather.2.cloned.1.call-start = ((), (), s32[]{:S(2)}) async-start(), calls=%async_computation.1 | async-start | bytes 8650752 | tf_op jit(solution)/shard_map/all_gather | solution.py:20
  7.3 295.1 %reduce-scatter.2.cloned.1.call-start = ((), (), s32[]{:S(2)}) async-start(), calls=%async_computation.2 | async-start | bytes 1114112 | tf_op jit(solution)/shard_map/reduce_scatter | solution.py:22
Sparse Core Ops, SparseCore 0:
  9.5 78.9 all-gather.1
  96.7 205.6 reduce-scatter.1
where the time goes:
time: 311 us
  waiting for transfers between devices  283 us (91%)
  between operations  13.4 us (4%)
  matrix products  7.99 us (3%)
  other arithmetic  4.25 us (1%)
    reduce_scatter x1, waiting for transfers between devices, per_device(): lax.psum_scatter(lax.dot_general(int_sym, flat_amp, (((1,), (1,)), ((), (...  206 us
    all_gather x1, waiting for transfers between devices, per_device(): gathered = lax.all_gather(integrals, 'va', axis=0, tiled=True)  76.8 us
    dot_general x1, matrix products, per_device(): lax.dot_general(int_sym, flat_amp, (((1,), (1,)), ((), ())), preferred_el...  7.99 us
  transfers between devices with their start and end apart: 2, of which 2 were waited for; matrix products, arithmetic and copies ran while one was open for 1% of the time, Pallas kernels for 0%

commit v1 on v0

--- a/solution.py
+++ b/solution.py
@@ -17,7 +17,9 @@
     )
     flat_amp = amp_sym.reshape(a_rows * slab_count, pair_local)
     row_tag = jnp.bitwise_xor(irrep_virt, irrep_occ[0])
-    gathered = lax.all_gather(integrals, "va", axis=0, tiled=True)
+    gathered = jnp.concatenate(
+        lax.all_to_all(jnp.stack([integrals] * lax.axis_size("va")), "va", 0, 0), axis=0
+    )
     int_sym = jnp.where(row_tag[:, None] == pair_tag[None, :], gathered, jnp.zeros_like(gathered))
     summed = lax.psum_scatter(
         lax.dot_general(

time: 311 us -> 440 us (1.41)
  waiting for transfers between devices: 283 us -> 393 us
  starting transfers between devices: 0.04 us -> 10.5 us
  other arithmetic: 4.25 us -> 10.2 us
    all_to_all x0 -> x1, waiting for transfers between devices: none -> 183 us  [per_device(): lax.all_to_all(jnp.stack([integrals] * lax.axis_size('va')), 'va', 0, 0)]
    all_gather x1 -> x0, waiting for transfers between devices: 76.8 us -> none  [per_device(): gathered = lax.all_gather(integrals, 'va', axis=0, tiled=True)]
    all_to_all x0 -> x1, starting transfers between devices: none -> 10.5 us  [per_device(): lax.all_to_all(jnp.stack([integrals] * lax.axis_size('va')), 'va', 0, 0)]
    select_n x0 -> x1, other arithmetic: none -> 8.57 us  [per_device(): jnp.where(row_tag[:, None] == pair_tag[None, :], gathered, jnp.zeros_like...]
    another operation x0 -> x1, local copies, waits for them, and re-layouts: none -> 5.22 us  [per_device(): jnp.stack([integrals] * lax.axis_size('va'))]
    reduce_scatter x1, waiting for transfers between devices: 206 us -> 210 us  [per_device(): lax.psum_scatter(lax.dot_general(int_sym, flat_amp, (((1,), (1,)), ((), (...]
  transfers between devices with their start and end apart: 2 -> 2, of which waited for: 2 -> 2; matrix products, arithmetic and copies ran while one was open for 1% -> 0% of each run, Pallas kernels for 0% -> 0%
where the time goes in v1:
time: 440 us
  waiting for transfers between devices  393 us (89%)
  between operations  13.4 us (3%)
  starting transfers between devices  10.5 us (2%)
  other arithmetic  10.2 us (2%)
  matrix products  6.79 us (2%)
  local copies, waits for them, and re-layouts  5.53 us (1%)
    reduce_scatter x1, waiting for transfers between devices, per_device(): lax.psum_scatter(lax.dot_general(int_sym, flat_amp, (((1,), (1,)), ((), (...  210 us
    all_to_all x1, waiting for transfers between devices, per_device(): lax.all_to_all(jnp.stack([integrals] * lax.axis_size('va')), 'va', 0, 0)  183 us
    all_to_all x1, starting transfers between devices, per_device(): lax.all_to_all(jnp.stack([integrals] * lax.axis_size('va')), 'va', 0, 0)  10.5 us
  transfers between devices with their start and end apart: 2, of which 2 were waited for; matrix products, arithmetic and copies ran while one was open for 0% of the time, Pallas kernels for 0%

profile of v1, /device:TPU:8, one launch (start us, length us, event | category | flops | bytes accessed | tf_op | source)
XLA Modules:
  0.0 439.7 jit_solution(11531956929320558907)
XLA Ops:
  6.5 5.2 %stack.2 = bf16[32,32,4096]{2,1,0:T(8,128)(2,1)} broadcast(bf16[32,4096]{1,0:T(8,128)(2,1)} %param.6), dimensions={1,2} | broadcast | bytes 8650752 | tf_op jit(solution)/shard_map/stack | solution.py:21
  11.8 0.0 copy-start
  11.8 0.0 copy-start.1
  11.8 0.0 copy-start.2
  11.8 10.5 %all-to-all-start = ((bf16[32,32,4096]{2,1,0:T(8,128)(2,1)}), bf16[32,32,4096]{2,1,0:T(8,128)(2,1)}, u32[]{:S(2)}, u32[]{:S(2)}) async-start(bf16[32,32,4096]{2,1,0:T(8,128)(2,1)} %stack.2), calls=%async_computation | async-start | bytes 16777216 | tf_op jit(solution)/shard_map/all_to_all | solution.py:21
  22.3 0.0 reduce-scatter.2.cloned.1.call-start
  22.3 0.0 copy-done
  22.3 0.1 dynamic_slice.6
  22.4 0.0 copy-done.1
  22.4 0.1 broadcast_xor_fusion
  22.5 0.1 xor.52
  22.6 0.1 eq.29
  22.7 0.1 dynamic_slice.7
  22.8 0.0 copy-done.2
  22.8 0.1 broadcast_xor_fusion.1
  22.8 0.0 copy-start.3
  22.8 182.7 %all-to-all-done = bf16[32,32,4096]{2,1,0:T(8,128)(2,1)} async-done(((bf16[32,32,4096]{2,1,0:T(8,128)(2,1)}), bf16[32,32,4096]{2,1,0:T(8,128)(2,1)}, u32[]{:S(2)}, u32[]{:S(2)}) %all-to-all-start) | async-done | bytes 8388640 | tf_op jit(solution)/shard_map/all_to_all | solution.py:21
  205.6 8.6 %compare_select_fusion = bf16[32,32,4096]{2,1,0:T(8,128)(2,1)} fusion(bf16[32,32,4096]{2,1,0:T(8,128)(2,1)} %all-to-all-done, s32[4096]{0:T(1024)S(1)} %xor.52, s32[32,32]{1,0:T(8,128)S(1)} %eq.29), kind=kLoop, calls=%fused_computation | loop fusion | flops 8388608 | bytes 16797696 | tf_op jit(solution)/shard_map/jit(_where)/select_n | solution.py:23
  214.1 0.0 copy-done.3
  214.1 6.8 %fusion.1 = f32[1024,256]{1,0:T(8,128)} fusion(bf16[1024,4096]{1,0:T(8,128)(2,1)} %bitcast.7, bf16[32,8,4096]{2,1,0:T(8,128)(2,1)S(1)} %copy-done.3, s32[4096]{0:T(1024)S(1)} %xor.52, s32[32,8]{1,0:T(8,128)S(1)} %broadcast_xor_fusion.1), kind=kOutput, calls=%fused_computation.3 | convolution fusion | flops 2149580800 | bytes 11551744 | tf_op jit(solution)/shard_map/dot_general | solution.py:25
  220.9 0.0 reduce-scatter.2.cloned.1.call-update
  221.0 210.4 %reduce-scatter.2.cloned.1.call-done = f32[64,256]{1,0:T(8,128)} async-done(((f32[1024,256]{1,0:T(8,128)}), f32[64,256]{1,0:T(8,128)}) %reduce-scatter.2.cloned.1.call-update) | async-done | bytes 65552 | tf_op jit(solution)/shard_map/reduce_scatter | solution.py:24
  431.4 1.5 convert_element_type.3
  (1 shorter events, 0.0 us)
Async XLA Ops:
  11.8 10.6 %copy-start = (s32[1024]{0:T(1024)S(1)}, s32[1024]{0:T(1024)}, u32[]{:S(2)}) copy-start(s32[1024]{0:T(1024)} %param.7) | copy-start | bytes 12292
  11.8 10.7 %copy-start.1 = (s32[64]{0:T(128)S(1)}, s32[64]{0:T(128)}, u32[]{:S(2)}) copy-start(s32[64]{0:T(128)} %param.8) | copy-start | bytes 772
  11.8 11.0 %copy-start.2 = (s32[8]{0:T(128)S(1)}, s32[8]{0:T(128)}, u32[]{:S(2)}) copy-start(s32[8]{0:T(128)} %param.9) | copy-start | bytes 100
  11.8 193.8 %all-to-all-start = ((bf16[32,32,4096]{2,1,0:T(8,128)(2,1)}), bf16[32,32,4096]{2,1,0:T(8,128)(2,1)}, u32[]{:S(2)}, u32[]{:S(2)}) async-start(bf16[32,32,4096]{2,1,0:T(8,128)(2,1)} %stack.2), calls=%async_computation | async-start | bytes 16777216 | tf_op jit(solution)/shard_map/all_to_all | solution.py:21
  22.3 409.1 %reduce-scatter.2.cloned.1.call-start = ((), (), s32[]{:S(2)}) async-start(), calls=%async_computation.2 | async-start | bytes 1114112 | tf_op jit(solution)/shard_map/reduce_scatter | solution.py:24
  22.8 191.3 %copy-start.3 = (bf16[32,8,4096]{2,1,0:T(8,128)(2,1)S(1)}, bf16[32,8,4096]{2,1,0:T(8,128)(2,1)}, u32[]{:S(2)}) copy-start(bf16[32,8,4096]{2,1,0:T(8,128)(2,1)} %param.5) | copy-start | bytes 6291460
Sparse Core Ops, SparseCore 0:
  221.1 210.2 reduce-scatter.1
